TPU v7x, 512 devices: a whole 4x8x8 slice. The times are simulated.
512 devices in a mesh: item: 8 (over y), rows: 32 (over z, x_hi, core), hid: 2 (over x_lo).
Axes of the slice: x: 4 (x_hi: 2, x_lo: 2; x = x_hi * 2 + x_lo), y: 8, z: 8, core: 2. Of those that a mesh axis runs over, the one named last changes fastest.
Arguments:
- latents: float32 [16, 32, 2048], P('item', 'rows'), may hold values from -6 to 6
- heights: int32 [16], P('item'), may hold values from 8 to 32, as said below
- widths: int32 [16], P('item'), may hold values from 8 to 32, as said below
- slot_item: int32 [16], P('item'), may hold values from 0 to 15, each once
- step_index: int32 [1], replicated, may hold values from 0 to 27
- cond_table: float32 [16, 5, 1536], replicated, may hold values from -9 to 9
- text_kv: bfloat16 [16, 2, 154, 768], P('item', None, None, 'hid'), may hold values from -175 to 175
- patch_weight: bfloat16 [64, 1536], replicated, may hold values from -0.75 to 0.75
- qkv_weight: bfloat16 [3, 1536, 768], P(None, ('item', 'rows'), 'hid'), may hold values from -0.15625 to 0.15625
- out_weight: bfloat16 [768, 1536], P('hid', ('item', 'rows')), may hold values from -0.21875 to 0.21875
- final_weight: bfloat16 [1536, 64], replicated, may hold values from -0.15625 to 0.15625
Outputs:
- next_latents: float32 [16, 32, 2048], P('item', 'rows')
- denoised: float32 [16, 32, 2048], P('item', 'rows')
Inputs may be any that keep to these rules, and one draw needn't show every extreme that they name: `heights`: every grid has at least 8 rows, and some item has exactly 32. `widths`: every grid has at least 8 columns, and some item has exactly 32. `slot_item`: each request is served by exactly one slot.
All inputs are finite; a program needn't handle non-finite values.
Results may differ from a plain program's by a relative error of at most 0.007.
Values may be sent and summed in bfloat16 or wider, within the bound.
A program may use at most 64 MiB of HBM per device.

v0:
```python
import jax
import jax.numpy as jnp
from jax import lax
from jax.sharding import PartitionSpec as P

HD = 64
STEPS = 28


def sigma_level(position):
    fraction = 1.0 - position / STEPS
    return 3.0 * fraction / (1.0 + 2.0 * fraction)


def position_embed(row_pos, col_count, model_width):
    quarter = model_width // 4
    frequency = 1.0 / 10000.0 ** (jnp.arange(quarter, dtype=jnp.float32) / quarter)
    col_pos = jnp.arange(col_count, dtype=jnp.float32)
    row_angle = row_pos[:, None] * frequency[None, :]
    col_angle = col_pos[:, None] * frequency[None, :]
    row_part = jnp.concatenate([jnp.sin(row_angle), jnp.cos(row_angle)], 1)
    col_part = jnp.concatenate([jnp.sin(col_angle), jnp.cos(col_angle)], 1)
    row_full = jnp.broadcast_to(
        row_part[:, None, :], (row_pos.shape[0], col_count, model_width // 2)
    )
    col_full = col_part[None, :, :]
    return jnp.concatenate([row_full, col_full], 2)


def normalize(values):
    mean_rows = jnp.mean(values, -1, keepdims=True)
    centered = values - mean_rows
    return centered * lax.rsqrt(jnp.mean(centered * centered, -1, keepdims=True) + 1e-06)


def body(
    latents,
    heights,
    widths,
    slot_item,
    step_index,
    cond_table,
    text_kv,
    patch_weight,
    qkv_weight,
    out_weight,
    final_weight,
):
    slot_count = latents.shape[0]
    rows_here = latents.shape[1]
    channels = patch_weight.shape[0]
    model_width = patch_weight.shape[1]
    col_count = latents.shape[2] // channels
    local_width = text_kv.shape[3]
    heads_here = local_width // HD
    text_count = text_kv.shape[2]
    per_slot = rows_here * col_count
    tok_rows = slot_count * per_slot
    row_start = lax.axis_index("rows") * rows_here
    row_pos = (row_start + jnp.arange(rows_here, dtype=jnp.int32)).astype(jnp.float32)
    patches = latents.reshape(tok_rows, channels).astype(jnp.bfloat16)
    embedded = jnp.dot(patches, patch_weight, preferred_element_type=jnp.float32).reshape(
        slot_count, per_slot, model_width
    )
    embedded = embedded + position_embed(row_pos, col_count, model_width)
    entries = cond_table.shape[0]
    chosen = (slot_item[:, None] == jnp.arange(entries, dtype=jnp.int32)[None, :]).astype(
        jnp.float32
    )
    conditions = jnp.dot(
        chosen, cond_table.reshape(entries, 5 * model_width), precision=lax.Precision.HIGHEST
    )
    conditions = conditions.reshape(slot_count, 5, model_width)
    normed = (normalize(embedded) * (1.0 + conditions[:, 1:2, :]) + conditions[:, 0:1, :]).astype(
        jnp.bfloat16
    )
    flat_rows = normed.reshape(tok_rows, model_width)
    projected = jnp.einsum(
        "td,kdh->kth",
        flat_rows,
        lax.all_gather(qkv_weight, ("item", "rows"), axis=1, tiled=True),
        preferred_element_type=jnp.float32,
    )
    projected = projected.astype(jnp.bfloat16)
    queries = projected[0].reshape(slot_count, per_slot, heads_here, HD)
    image_kv = projected[1:].reshape(2, slot_count, rows_here, col_count, local_width)
    score_scale = HD ** (-0.5)
    text_keys = text_kv[:, 0].reshape(slot_count, text_count, heads_here, HD)
    text_vals = text_kv[:, 1].reshape(slot_count, text_count, heads_here, HD)
    text_score = (
        jnp.einsum("sqhd,skhd->shqk", queries, text_keys, preferred_element_type=jnp.float32)
        * score_scale
    )
    first_top = jnp.max(text_score, -1)
    text_weights = jnp.exp(text_score - first_top[..., None])
    first_total = jnp.sum(text_weights, -1)
    first_acc = jnp.einsum(
        "shqk,skhd->shqd",
        text_weights.astype(jnp.bfloat16),
        text_vals,
        preferred_element_type=jnp.float32,
    )
    col_live = jnp.arange(col_count, dtype=jnp.int32)[None, :] < widths[:, None]
    gathered = lax.all_gather(image_kv, "rows", axis=2, tiled=True)
    run_top = first_top
    run_total = first_total
    run_acc = first_acc
    key_rows = gathered.shape[2]
    key_piece = gathered[0].reshape(slot_count, key_rows * col_count, heads_here, HD)
    val_piece = gathered[1].reshape(slot_count, key_rows * col_count, heads_here, HD)
    scores = (
        jnp.einsum("sqhd,skhd->shqk", queries, key_piece, preferred_element_type=jnp.float32)
        * score_scale
    )
    key_index = jnp.arange(key_rows, dtype=jnp.int32)
    live_mask = (key_index[None, :, None] < heights[:, None, None]) & col_live[:, None, :]
    live_mask = live_mask.reshape(slot_count, 1, 1, key_rows * col_count)
    scores = jnp.where(live_mask, scores, -1e30)
    new_top = jnp.maximum(run_top, jnp.max(scores, -1))
    factor = jnp.exp(run_top - new_top)
    weights = jnp.exp(scores - new_top[..., None])
    run_total = run_total * factor + jnp.sum(weights, -1)
    run_acc = run_acc * factor[..., None] + jnp.einsum(
        "shqk,skhd->shqd",
        weights.astype(jnp.bfloat16),
        val_piece,
        preferred_element_type=jnp.float32,
    )
    run_top, run_total, run_acc = (new_top, run_total, run_acc)
    attended = (
        (run_acc / run_total[..., None])
        .transpose(0, 2, 1, 3)
        .reshape(tok_rows, local_width)
        .astype(jnp.bfloat16)
    )
    partial_value = jnp.dot(
        attended,
        lax.all_gather(out_weight, ("item", "rows"), axis=1, tiled=True),
        preferred_element_type=jnp.float32,
    )
    summed = lax.psum(partial_value.astype(jnp.bfloat16), "hid").astype(jnp.float32)
    summed = summed.reshape(slot_count, per_slot, model_width)
    residual = embedded + conditions[:, 2:3, :] * summed
    final_in = (normalize(residual) * (1.0 + conditions[:, 4:5, :]) + conditions[:, 3:4, :]).astype(
        jnp.bfloat16
    )
    velocity = jnp.dot(
        final_in.reshape(tok_rows, model_width), final_weight, preferred_element_type=jnp.float32
    )
    position = step_index[0].astype(jnp.float32)
    sigma_now = sigma_level(position)
    sigma_next = sigma_level(position + 1.0)
    row_global = row_start + jnp.arange(rows_here, dtype=jnp.int32)
    live_patch = (row_global[None, :, None] < heights[:, None, None]) & col_live[:, None, :]
    velocity = velocity.reshape(slot_count, rows_here, col_count, channels)
    live_velocity = jnp.where(live_patch[..., None], velocity, 0.0).reshape(
        slot_count, rows_here, col_count * channels
    )
    next_latents = latents + (sigma_next - sigma_now) * live_velocity
    denoised = latents - sigma_now * live_velocity
    return (next_latents, denoised)


def solution(mesh):
    return jax.shard_map(
        body,
        mesh=mesh,
        in_specs=(
            P("item", "rows", None),
            P("item"),
            P("item"),
            P("item"),
            P(),
            P(),
            P("item", None, None, "hid"),
            P(),
            P(None, ("item", "rows"), "hid"),
            P("hid", ("item", "rows")),
            P(),
        ),
        out_specs=(P("item", "rows", None), P("item", "rows", None)),
        check_vma=False,
    )
```

profile of v0, /device:TPU:1, one launch (start us, length us, event | category | flops | bytes accessed | tf_op | source)
XLA Modules:
  0.0 422.9 jit_solution(1402297968687768749)
XLA Ops:
  7.2 0.0 all-gather.5.cloned.1.call-start
  7.2 1.4 copy.35
  8.6 0.0 all-gather.5.cloned.1.call-update
  8.6 0.0 all-gather.9.cloned.1.call-start
  8.7 0.7 all-gather.9.cloned.1.call-update
  9.4 0.0 all-gather.7.cloned.1.call-start
  9.5 0.1 fusion.49
  9.5 0.2 fusion.42
  9.8 0.8 convert_reduce_fusion
  10.6 0.1 convert_element_type.46
  10.7 1.2 fusion.56
  11.9 0.2 multiply_reduce_fusion.1
  12.1 0.3 fusion.25
  12.4 0.1 add_convert_fusion.1
  12.6 136.8 %all-gather.5.cloned.1.call-done = bf16[3,1536,384]{2,0,1:T(4,128)(2,1)} async-done(((bf16[3,6,384]{2,0,1:T(4,128)(2,1)}), bf16[3,1536,384]{2,0,1:T(4,128)(2,1)}) %all-gather.5.cloned.1.call-update) | async-done | bytes 3538960 | tf_op jit(solution)/shard_map/all_gather | solution.py:81
  149.4 3.1 fusion.20
  152.5 0.6 slice.48
  153.1 0.0 all-gather.7.cloned.1.call-update
  153.2 0.0 all-reduce.2.cloned.1.call-start
  153.2 0.1 broadcast_and_fusion.1
  153.3 0.1 broadcast_and_fusion
  153.4 0.1 and.40
  153.5 0.7 fusion.54
  154.2 0.5 copy.37
  154.7 0.5 copy.39
  155.2 109.8 %all-gather.9.cloned.1.call-done = bf16[256,6,384]{2,1,0:T(8,128)(2,1)} async-done(((bf16[1,6,384]{2,1,0:T(8,128)(2,1)}), bf16[256,6,384]{2,1,0:T(8,128)(2,1)}) %all-gather.9.cloned.1.call-update) | async-done | bytes 1179664 | tf_op jit(solution)/shard_map/all_gather | solution.py:138
  265.0 3.3 reshape.279
  268.3 0.1 reshape_squeeze.15
  268.4 0.3 fusion.57
  268.7 0.2 fusion.28
  268.9 85.4 %all-gather.7.cloned.1.call-done = bf16[2,2,32,32,384]{4,3,2,1,0:T(8,128)(2,1)} async-done(((bf16[2,2,1,32,384]{4,3,2,1,0:T(8,128)(2,1)}), bf16[2,2,32,32,384]{4,3,2,1,0:T(8,128)(2,1)}) %all-gather.7.cloned.1.call-update) | async-done | bytes 3145744 | tf_op jit(solution)/shard_map/all_gather | solution.py:104
  354.4 3.5 fusion.53
  357.8 3.7 reshape_squeeze.18
  361.6 3.4 fusion.58
  365.0 5.9 %reshape_squeeze.19 = bf16[2,1024,6,64]{3,2,1,0:T(8,128)(2,1)} reshape(bf16[1,2,32,32,384]{4,3,2,1,0:T(8,128)(2,1)} %get-tuple-element.5) | data formatting | bytes 3145728 | tf_op jit(solution)/shard_map/reshape;squeeze | solution.py:110
  370.9 0.4 fusion.8
  371.3 3.3 fusion.16
  374.6 0.3 fusion.19
  375.0 0.1 convert_element_type.54
  375.1 0.7 copy-done.1
  375.9 1.2 convolution_convert_fusion
  377.8 34.3 %all-reduce.2.cloned.1.call-done = bf16[2,32,1536]{2,1,0:T(8,128)(2,1)} async-done(((bf16[2,32,1536]{2,1,0:T(8,128)(2,1)}), bf16[2,32,1536]{2,1,0:T(8,128)(2,1)}) %all-reduce.2.cloned.1.call-update) | async-done | bytes 196624 | tf_op jit(solution)/shard_map/psum | solution.py:141
  412.1 1.1 fusion.38
  413.2 1.1 multiply_reduce_fusion
  414.3 1.2 broadcast_multiply_fusion
  415.5 0.1 mul.213
  415.6 0.1 mul.214
  415.7 0.6 fusion.55
  (31 shorter events, 0.2 us)
Async XLA Ops:
  7.2 4.9 %copy-start = (f32[16,5,1536]{2,0,1:T(8,128)S(1)}, f32[16,5,1536]{2,0,1:T(8,128)}, u32[]{:S(2)}) copy-start(f32[16,5,1536]{2,0,1:T(8,128)} %param.16) | copy-start | bytes 1474564
  7.2 4.9 %copy-start.4 = (s32[2]{0:T(128)S(1)}, s32[2]{0:T(128)}, u32[]{:S(2)}) copy-start(s32[2]{0:T(128)} %param.14) | copy-start | bytes 28
  7.2 142.2 %all-gather.5.cloned.1.call-start = ((), (), s32[]{:S(2)}) async-start(), calls=%async_computation | async-start | bytes 4737024 | tf_op jit(solution)/shard_map/all_gather | solution.py:81
  8.6 256.3 %all-gather.9.cloned.1.call-start = ((), (), s32[]{:S(2)}) async-start(), calls=%async_computation.3 | async-start | bytes 1579008 | tf_op jit(solution)/shard_map/all_gather | solution.py:138
  9.4 345.0 %all-gather.7.cloned.1.call-start = ((), (), s32[]{:S(2)}) async-start(), calls=%async_computation.1 | async-start | bytes 3244032 | tf_op jit(solution)/shard_map/all_gather | solution.py:104
  149.4 3.9 copy-start.5
  149.4 3.9 copy-start.6
  149.4 4.1 copy-start.2
  153.2 258.9 %all-reduce.2.cloned.1.call-start = ((), (), s32[]{:S(2)}) async-start(), calls=%async_computation.2 | async-start | bytes 393216 | tf_op jit(solution)/shard_map/psum | solution.py:141
  374.6 1.3 copy-start.1
  375.0 39.3 %copy-start.7 = (bf16[1536,64]{0,1:T(8,128)(2,1)S(1)}, bf16[1536,64]{0,1:T(8,128)(2,1)}, u32[]{:S(2)}) copy-start(bf16[1536,64]{0,1:T(8,128)(2,1)} %param.21) | copy-start | bytes 589828
  377.0 38.7 %copy-start.3 = (f32[2,1,2048]{2,1,0:T(1,128)S(1)}, f32[2,1,2048]{2,1,0:T(1,128)}, u32[]{:S(2)}) copy-start(f32[2,1,2048]{2,1,0:T(1,128)} %param.11) | copy-start | bytes 49156
Sparse Core Ops, SparseCore 0:
  12.5 136.7 all-gather.4
  153.5 111.3 all-gather.8
  268.3 86.0 all-gather.6
  377.2 34.8 all-reduce.1
where the time goes:
time: 423 us
  waiting for transfers between devices  367 us (87%)
  local copies, waits for them, and re-layouts  21.5 us (5%)
  between operations  14.8 us (3%)
  matrix products  14.3 us (3%)
  other arithmetic  5.08 us (1%)
    all_gather x1, waiting for transfers between devices, body(): lax.all_gather(qkv_weight, ('item', 'rows'), axis=1, tiled=True)  137 us
    all_gather x1, waiting for transfers between devices, body(): lax.all_gather(out_weight, ('item', 'rows'), axis=1, tiled=True)  110 us
    all_gather x1, waiting for transfers between devices, body(): gathered = lax.all_gather(image_kv, 'rows', axis=2, tiled=True)  85.4 us
    psum x1, waiting for transfers between devices, body(): lax.psum(partial_value.astype(jnp.bfloat16), 'hid').astype(jnp.float32)  34.3 us
  transfers between devices with their start and end apart: 4, of which 4 were waited for; matrix products, arithmetic and copies ran while one was open for 3% of the time, Pallas kernels for 0%

commit v1 on v0

--- a/solution.py
+++ b/solution.py
@@ -5,6 +5,13 @@
 
 HD = 64
 STEPS = 28
+
+
+def exchange_gather(x, name, d):
+    peers = lax.axis_size(name)
+    pieces = jnp.stack([x for _ in range(peers)])
+    pieces = lax.all_to_all(pieces, name, split_axis=0, concat_axis=0)
+    return jnp.concatenate(pieces, axis=d)
 
 
 def sigma_level(position):
@@ -135,7 +142,7 @@
     )
     partial_value = jnp.dot(
         attended,
-        lax.all_gather(out_weight, ("item", "rows"), axis=1, tiled=True),
+        exchange_gather(out_weight, ("item", "rows"), 1),
         preferred_element_type=jnp.float32,
     )
     summed = lax.psum(partial_value.astype(jnp.bfloat16), "hid").astype(jnp.float32)

time: 423 us -> 337 us (0.80)
  waiting for transfers between devices: 367 us -> 265 us
  starting transfers between devices: 0.16 us -> 11.4 us
    all_gather x1 -> x0, waiting for transfers between devices: 110 us -> none  [body(): lax.all_gather(out_weight, ('item', 'rows'), axis=1, tiled=True)]
    all_to_all x0 -> x1, waiting for transfers between devices: none -> 37.9 us  [exchange_gather(): pieces = lax.all_to_all(pieces, name, split_axis=0, concat_axis=0)]
    all_gather x1, waiting for transfers between devices: 85.4 us -> 56.1 us  [body(): gathered = lax.all_gather(image_kv, 'rows', axis=2, tiled=True)]
    all_to_all x0 -> x1, starting transfers between devices: none -> 11.1 us  [exchange_gather(): pieces = lax.all_to_all(pieces, name, split_axis=0, concat_axis=0)]
  transfers between devices with their start and end apart: 4 -> 4, of which waited for: 4 -> 4; matrix products, arithmetic and copies ran while one was open for 3% -> 4% of each run, Pallas kernels for 0% -> 0%
where the time goes in v1:
time: 337 us; the launch traced here: 336 us
  waiting for transfers between devices  265 us (79%)
  local copies, waits for them, and re-layouts  24.3 us (7%)
  between operations  14.8 us (4%)
  matrix products  14.3 us (4%)
  starting transfers between devices  11.4 us (3%)
  other arithmetic  6.17 us (2%)
    all_gather x1, waiting for transfers between devices, body(): lax.all_gather(qkv_weight, ('item', 'rows'), axis=1, tiled=True)  137 us
    all_gather x1, waiting for transfers between devices, body(): gathered = lax.all_gather(image_kv, 'rows', axis=2, tiled=True)  56.1 us
    all_to_all x1, waiting for transfers between devices, exchange_gather(): pieces = lax.all_to_all(pieces, name, split_axis=0, concat_axis=0)  37.9 us
    psum x1, waiting for transfers between devices, body(): lax.psum(partial_value.astype(jnp.bfloat16), 'hid').astype(jnp.float32)  34.3 us
    all_to_all x1, starting transfers between devices, exchange_gather(): pieces = lax.all_to_all(pieces, name, split_axis=0, concat_axis=0)  11.1 us
  transfers between devices with their start and end apart: 4, of which 4 were waited for; matrix products, arithmetic and copies ran while one was open for 4% of the time, Pallas kernels for 0%

profile of v1, /device:TPU:1, one launch (start us, length us, event | category | flops | bytes accessed | tf_op | source)
XLA Modules:
  0.0 336.4 jit_solution(720831609192284192)
XLA Ops:
  7.2 0.0 all-gather.3.cloned.1.call-start
  7.2 1.4 copy.36
  8.6 0.0 all-gather.3.cloned.1.call-update
  8.6 0.0 all-gather.5.cloned.1.call-start
  8.7 0.8 convert_reduce_fusion
  9.5 0.1 convert_element_type.46
  9.6 0.1 fusion.49
  9.7 0.2 fusion.42
  9.9 1.2 fusion.56
  11.1 0.2 multiply_reduce_fusion.1
  11.4 0.3 fusion.25
  11.7 0.6 slice_bitcast_fusion.2
  12.3 0.1 add_convert_fusion.1
  12.4 136.9 %all-gather.3.cloned.1.call-done = bf16[3,1536,384]{2,0,1:T(4,128)(2,1)} async-done(((bf16[3,6,384]{2,0,1:T(4,128)(2,1)}), bf16[3,1536,384]{2,0,1:T(4,128)(2,1)}) %all-gather.3.cloned.1.call-update) | async-done | bytes 3538960 | tf_op jit(solution)/shard_map/all_gather | solution.py:88
  149.4 3.1 fusion.20
  152.4 0.6 slice.48
  153.1 1.3 stack.2
  154.4 11.1 %all-to-all-start = ((bf16[256,384,6]{1,2,0:T(8,128)(2,1)}), bf16[256,384,6]{1,2,0:T(8,128)(2,1)S(1)}, u32[]{:S(2)}, u32[]{:S(2)}) async-start(bf16[256,384,6]{1,2,0:T(8,128)(2,1)} %stack.2), calls=%async_computation | async-start | bytes 3145728 | tf_op jit(solution)/shard_map/all_to_all | solution.py:13
  165.6 0.2 all-reduce.2.cloned.1.call-start
  165.8 0.6 broadcast_and_fusion.1
  166.4 0.1 broadcast_and_fusion
  166.5 0.7 and.40
  167.2 1.5 fusion.54
  168.6 2.0 copy.38
  170.6 1.2 copy.40
  171.8 37.9 %all-to-all-done = bf16[256,384,6]{1,2,0:T(8,128)(2,1)S(1)} async-done(((bf16[256,384,6]{1,2,0:T(8,128)(2,1)}), bf16[256,384,6]{1,2,0:T(8,128)(2,1)S(1)}, u32[]{:S(2)}, u32[]{:S(2)}) %all-to-all-start) | async-done | bytes 1179680 | tf_op jit(solution)/shard_map/all_to_all | solution.py:13
  209.7 1.2 reshape.275
  211.0 0.1 reshape_squeeze.15
  211.1 0.3 fusion.57
  211.4 0.2 fusion.28
  211.6 56.1 %all-gather.5.cloned.1.call-done = bf16[2,2,32,32,384]{4,3,2,1,0:T(8,128)(2,1)} async-done(((bf16[2,2,1,32,384]{4,3,2,1,0:T(8,128)(2,1)}), bf16[2,2,32,32,384]{4,3,2,1,0:T(8,128)(2,1)}) %all-gather.5.cloned.1.call-update) | async-done | bytes 3145744 | tf_op jit(solution)/shard_map/all_gather | solution.py:111
  267.8 3.5 %fusion.53 = (bf16[1,2,32,32,384]{4,3,2,1,0:T(8,128)(2,1)S(1)}, bf16[1,2,32,32,384]{4,3,2,1,0:T(8,128)(2,1)}) fusion(bf16[2,2,32,32,384]{4,3,2,1,0:T(8,128)(2,1)} %all-gather.5.cloned.1.call-done), kind=kLoop, calls=%fused_computation.81 | loop fusion | bytes 6291456 | tf_op jit(solution)/shard_map/slice | solution.py:116
  271.3 3.7 %reshape_squeeze.18 = bf16[2,1024,6,64]{3,2,1,0:T(8,128)(2,1)} reshape(bf16[1,2,32,32,384]{4,3,2,1,0:T(8,128)(2,1)S(1)} %get-tuple-element.4) | data formatting | bytes 3145728 | tf_op jit(solution)/shard_map/reshape;squeeze | solution.py:116
  275.0 3.4 %fusion.58 = (f32[2,6,32]{2,1,0:T(8,128)S(1)}, f32[2,6,32,1024]{3,2,1,0:T(8,128)S(1)}) fusion(bf16[2,1024,6,64]{3,2,1,0:T(8,128)(2,1)} %reshape_squeeze.18, bf16[2,32,6,64]{3,2,1,0:T(8,128)(2,1)S(1)} %reshape_squeeze.15, pred[2,1024]{1,0:T(4,128)(4,1)S(1)} %copy-done.7), kind=kOutput, calls=%fused_computation.86 | convolution fusion | flops 51510912 | bytes 3198464 | tf_op jit(solution)/shard_map/sqhd,skhd->shqk/dot_general | solution.py:119
  278.4 5.9 %reshape_squeeze.19 = bf16[2,1024,6,64]{3,2,1,0:T(8,128)(2,1)} reshape(bf16[1,2,32,32,384]{4,3,2,1,0:T(8,128)(2,1)} %get-tuple-element.5) | data formatting | bytes 3145728 | tf_op jit(solution)/shard_map/reshape;squeeze | solution.py:117
  284.3 0.4 fusion.8
  284.7 3.4 %fusion.16 = f32[2,32,6,64]{3,1,2,0:T(8,128)S(1)} fusion(bf16[2,1024,6,64]{3,2,1,0:T(8,128)(2,1)} %reshape_squeeze.19, f32[2,6,32,1024]{3,2,1,0:T(8,128)S(1)} %get-tuple-element.26, f32[2,6,32]{2,1,0:T(8,128)S(1)} %max.18), kind=kOutput, calls=%fused_computation.18 | convolution fusion | flops 51118080 | bytes 3245568 | tf_op jit(solution)/shard_map/shqk,skhd->shqd/dot_general | solution.py:130
  288.1 0.3 fusion.19
  288.6 0.1 convert_element_type.54
  288.7 0.7 copy-done.1
  289.4 1.2 convolution_convert_fusion
  291.3 34.3 %all-reduce.2.cloned.1.call-done = bf16[2,32,1536]{2,1,0:T(8,128)(2,1)} async-done(((bf16[2,32,1536]{2,1,0:T(8,128)(2,1)}), bf16[2,32,1536]{2,1,0:T(8,128)(2,1)}) %all-reduce.2.cloned.1.call-update) | async-done | bytes 196624 | tf_op jit(solution)/shard_map/psum | solution.py:148
  325.6 1.1 fusion.38
  326.7 1.1 multiply_reduce_fusion
  327.9 1.2 broadcast_multiply_fusion
  329.1 0.1 mul.213
  329.2 0.1 mul.214
  329.3 0.6 fusion.55
  (47 shorter events, 0.3 us)
Async XLA Ops:
  7.2 4.2 %copy-start = (f32[16,5,1536]{2,0,1:T(8,128)S(1)}, f32[16,5,1536]{2,0,1:T(8,128)}, u32[]{:S(2)}) copy-start(f32[16,5,1536]{2,0,1:T(8,128)} %param.16) | copy-start | bytes 1474564
  7.2 4.2 %copy-start.11 = (s32[2]{0:T(128)S(1)}, s32[2]{0:T(128)}, u32[]{:S(2)}) copy-start(s32[2]{0:T(128)} %param.14) | copy-start | bytes 28
  7.2 142.2 %all-gather.3.cloned.1.call-start = ((), (), s32[]{:S(2)}) async-start(), calls=%async_computation.1 | async-start | bytes 4737024 | tf_op jit(solution)/shard_map/all_gather | solution.py:88
  8.6 259.1 %all-gather.5.cloned.1.call-start = ((), (), s32[]{:S(2)}) async-start(), calls=%async_computation.2 | async-start | bytes 3244032 | tf_op jit(solution)/shard_map/all_gather | solution.py:111
  149.4 3.8 %copy-start.10 = (bf16[384,6]{0,1:T(8,128)(2,1)S(1)}, bf16[384,6]{0,1:T(8,128)(2,1)}, u32[]{:S(2)}) copy-start(bf16[384,6]{0,1:T(8,128)(2,1)} %param.20) | copy-start | bytes 13828
  154.4 11.4 %copy-start.12 = (s32[2]{0:T(128)S(1)}, s32[2]{0:T(128)}, u32[]{:S(2)}) copy-start(s32[2]{0:T(128)} %param.12) | copy-start | bytes 28
  154.4 11.4 %copy-start.13 = (s32[2]{0:T(128)S(1)}, s32[2]{0:T(128)}, u32[]{:S(2)}) copy-start(s32[2]{0:T(128)} %param.13) | copy-start | bytes 28
  154.4 12.8 %copy-start.2 = (bf16[2,2,154,384]{3,1,2,0:T(2,128)(2,1)S(1)}, bf16[2,2,154,384]{3,1,2,0:T(2,128)(2,1)}, u32[]{:S(2)}) copy-start(bf16[2,2,154,384]{3,1,2,0:T(2,128)(2,1)} %param.17) | copy-start | bytes 1419268
  154.4 55.3 %all-to-all-start = ((bf16[256,384,6]{1,2,0:T(8,128)(2,1)}), bf16[256,384,6]{1,2,0:T(8,128)(2,1)S(1)}, u32[]{:S(2)}, u32[]{:S(2)}) async-start(bf16[256,384,6]{1,2,0:T(8,128)(2,1)} %stack.2), calls=%async_computation | async-start | bytes 3145728 | tf_op jit(solution)/shard_map/all_to_all | solution.py:13
  165.6 160.1 %all-reduce.2.cloned.1.call-start = ((), (), s32[]{:S(2)}) async-start(), calls=%async_computation.3 | async-start | bytes 393216 | tf_op jit(solution)/shard_map/psum | solution.py:148
  171.8 39.3 %copy-start.3 = (bf16[2,1,154,384]{2,3,0,1:T(8,128)(2,1)S(1)}, bf16[2,1,154,384]{2,3,0,1:T(8,128)(2,1)}, u32[]{:S(2)}) copy-start(bf16[2,1,154,384]{2,3,0,1:T(8,128)(2,1)} %copy.38) | copy-start | bytes 709636
  271.3 3.7 %copy-start.7 = (pred[2,1024]{1,0:T(4,128)(4,1)S(1)}, pred[2,1024]{1,0:T(4,128)(4,1)}, u32[]{:S(2)}) copy-start(pred[2,1024]{1,0:T(4,128)(4,1)} %and.40) | copy-start | bytes 6148
  284.7 3.4 %copy-start.4 = (bf16[2,1,154,384]{2,3,0,1:T(8,128)(2,1)S(1)}, bf16[2,1,154,384]{2,3,0,1:T(8,128)(2,1)}, u32[]{:S(2)}) copy-start(bf16[2,1,154,384]{2,3,0,1:T(8,128)(2,1)} %copy.40) | copy-start | bytes 709636
  288.1 1.3 copy-start.1
  288.1 37.5 %copy-start.5 = (f32[2,1536]{1,0:T(2,128)S(1)}, f32[2,1536]{1,0:T(2,128)}, u32[]{:S(2)}) copy-start(f32[2,1536]{1,0:T(2,128)} %get-tuple-element.8) | copy-start | bytes 36868
  288.5 39.3 %copy-start.8 = (f32[2,1536]{1,0:T(2,128)S(1)}, f32[2,1536]{1,0:T(2,128)}, u32[]{:S(2)}) copy-start(f32[2,1536]{1,0:T(2,128)} %get-tuple-element.9) | copy-start | bytes 36868
  288.5 39.3 %copy-start.9 = (f32[2,1536]{1,0:T(2,128)S(1)}, f32[2,1536]{1,0:T(2,128)}, u32[]{:S(2)}) copy-start(f32[2,1536]{1,0:T(2,128)} %get-tuple-element.10) | copy-start | bytes 36868
  288.5 39.3 %copy-start.14 = (pred[2,32]{1,0:T(4,128)(4,1)S(1)}, pred[2,32]{1,0:T(4,128)(4,1)}, u32[]{:S(2)}) copy-start(pred[2,32]{1,0:T(4,128)(4,1)} %get-tuple-element.19) | copy-start | bytes 196
  288.5 39.3 %copy-start.15 = (bf16[1536,64]{0,1:T(8,128)(2,1)S(1)}, bf16[1536,64]{0,1:T(8,128)(2,1)}, u32[]{:S(2)}) copy-start(bf16[1536,64]{0,1:T(8,128)(2,1)} %param.21) | copy-start | bytes 589828
  290.5 38.7 %copy-start.6 = (f32[2,1,2048]{2,1,0:T(1,128)S(1)}, f32[2,1,2048]{2,1,0:T(1,128)}, u32[]{:S(2)}) copy-start(f32[2,1,2048]{2,1,0:T(1,128)} %param.11) | copy-start | bytes 49156
Sparse Core Ops, SparseCore 0:
  12.5 136.7 all-gather.2
  153.2 114.5 all-gather.4
  290.7 34.8 all-reduce.1
